TPU v7x, 512 devices: a whole 4x8x8 slice. The times are simulated.
512 devices in a mesh: tm: 32 (over z, y_lo, core), depth: 16 (over x, y_hi).
Axes of the slice: x: 4, y: 8 (y_hi: 4, y_lo: 2; y = y_hi * 2 + y_lo), z: 8, core: 2. Of those that a mesh axis runs over, the one named last changes fastest.
Arguments:
- raw: bfloat16 [512, 128, 128], P('tm', 'depth'), may hold values from -6 to 6
- stream: bfloat16 [512, 128, 2048], P('tm', 'depth'), may hold values from -6 to 6
- conv_w: bfloat16 [3, 128, 2048], replicated, may hold values from -0.3125 to 0.3125
- gain: float32 [2048], replicated, may hold values from 0.1 to 1.9
- w_qkv: bfloat16 [2048, 3072], P('tm', 'depth'), may hold values from -4 to 4
- mask: int32 [16, 32, 5], P('depth', 'tm'), may hold values from 0 to 1, as said below
Outputs:
- context: bfloat16 [512, 128, 1024], P('tm', 'depth')
Inputs may be any that keep to these rules, and one draw needn't show every extreme that they name: mask[p, i, 2] = 1 for every block; mask[p, i, e] = 0 wherever i + e - 2 lies outside 0 to 31.
All inputs are finite; a program needn't handle non-finite values.
Results may differ from a plain program's by a relative error of at most 0.012.
The roundings to bfloat16 on the way count: a program that leaves them out, or rounds other values in their place, can miss the bound.
Values may be sent and summed in bfloat16 or wider, within the bound.
A program may use at most 64 MiB of HBM per device.

v0:
```python
import math

import jax
import jax.numpy as jnp
from jax import lax
from jax.sharding import PartitionSpec as P

HEADS = 8
HD = 128
BT = 16
PP = 8
RD = 2


def padded_2(value, sides, width):
    for axis, dim in sides:
        devices, length = (lax.axis_size(axis), value.shape[dim])
        up = [(i, (i + 1) % devices) for i in range(devices - 1)]
        down = [(j, i) for i, j in up]
        last = lax.slice_in_dim(value, length - width, length, axis=dim)
        leading = lax.slice_in_dim(value, 0, width, axis=dim)
        before = lax.ppermute(last, axis, up)
        after = lax.ppermute(leading, axis, down)
        value = jnp.concatenate([before, value, after], axis=dim)
    return value


def from_behind(value, axis, by):
    devices = lax.axis_size(axis)
    pairs = [(i, i + by) for i in range(devices) if 0 <= i + by < devices]
    return lax.ppermute(value, axis, pairs)


def head_attend(query_head, key_head, value_head, allowed):
    inv_root = 1.0 / math.sqrt(HD)
    scores = (
        jnp.einsum("qd,kd->qk", query_head, key_head, preferred_element_type=jnp.float32) * inv_root
    )
    scores = jnp.where(allowed, scores, -1e30)
    row_max = jnp.max(scores, axis=-1, keepdims=True)
    powers = jnp.exp(scores - row_max)
    weights = (powers / jnp.sum(powers, axis=-1, keepdims=True)).astype(jnp.bfloat16)
    return jnp.dot(weights, value_head, preferred_element_type=jnp.float32).astype(jnp.bfloat16)


def per_device(raw, stream, conv_w, gain, w_qkv, mask):
    time_len, site_len, feat_len = raw.shape
    tok_rows = time_len * site_len
    padded = padded_2(raw, (("depth", 1),), 1)
    embedded = stream.reshape(tok_rows, stream.shape[2]).astype(jnp.float32)
    for offset in range(3):
        window = padded[:, offset : offset + site_len].reshape(tok_rows, feat_len)
        embedded = embedded + jnp.dot(window, conv_w[offset], preferred_element_type=jnp.float32)
    normed = (
        embedded * lax.rsqrt(jnp.mean(embedded * embedded, axis=-1, keepdims=True) + 1e-05) * gain
    ).astype(jnp.bfloat16)
    columns = lax.all_gather(w_qkv, "depth", axis=1, tiled=True)
    projected = jnp.dot(
        normed,
        lax.all_gather(columns, "tm", axis=0, tiled=True),
        preferred_element_type=jnp.float32,
    ).astype(jnp.bfloat16)
    head_cols = projected.shape[1] // 3
    queries = projected[:, :head_cols]
    keyvals = projected[:, head_cols:]
    earlier = []
    later = []
    moving_back = keyvals
    moving_ahead = keyvals
    for hop_index in range(RD):
        moving_back = from_behind(moving_back, "tm", 1)
        moving_ahead = from_behind(moving_ahead, "tm", -1)
        earlier.insert(0, moving_back)
        later.append(moving_ahead)
    gathered = jnp.concatenate(earlier + [keyvals] + later, axis=0)
    block_rows = BT * PP
    own_blocks = tok_rows // block_rows
    span_blocks = gathered.shape[0] // block_rows
    local_mask = mask[0]
    query_ids = jnp.arange(own_blocks, dtype=jnp.int32)[:, None]
    key_ids = jnp.arange(span_blocks, dtype=jnp.int32)[None, :]
    entry_ids = key_ids - query_ids
    picks = entry_ids[:, :, None] == jnp.arange(local_mask.shape[1], dtype=jnp.int32)[None, None, :]
    block_allowed = jnp.sum(jnp.where(picks, local_mask[:, None, :], 0), axis=-1) > 0
    allowed = jnp.repeat(jnp.repeat(block_allowed, block_rows, axis=0), block_rows, axis=1)
    query_heads = queries.reshape(tok_rows, HEADS, HD).transpose(1, 0, 2)
    key_heads = gathered[:, :head_cols].reshape(gathered.shape[0], HEADS, HD).transpose(1, 0, 2)
    value_heads = gathered[:, head_cols:].reshape(gathered.shape[0], HEADS, HD).transpose(1, 0, 2)
    context = lax.map(
        lambda operands: head_attend(operands[0], operands[1], operands[2], allowed),
        (query_heads, key_heads, value_heads),
    )
    return context.transpose(1, 0, 2).reshape(time_len, site_len, head_cols)


def solution(mesh):
    in_specs = (
        P("tm", "depth", None),
        P("tm", "depth", None),
        P(),
        P(),
        P("tm", "depth"),
        P("depth", "tm", None),
    )
    out_specs = P("tm", "depth", None)
    return jax.shard_map(
        per_device, mesh=mesh, in_specs=in_specs, out_specs=out_specs, check_vma=False
    )
```

profile of v0, /device:TPU:1, one launch (start us, length us, event | category | flops | bytes accessed | tf_op | source)
XLA Modules:
  0.0 192.2 jit_solution(5119026603187726884)
XLA Ops:
  6.5 42.6 %all-gather = bf16[16,192,64]{1,2,0:T(8,128)(2,1)S(1)} all-gather(bf16[1,192,64]{1,2,0:T(8,128)(2,1)} %bitcast.82), channel_id=1, replica_groups=mesh['tm'=32,'depth'=16] {'depth'}, dimensions={0}, use_global_device_ids=true | all-gather | bytes 417792 | tf_op jit(solution)/shard_map/all_gather | solution.py:57
  49.1 0.3 copy.21
  49.4 1.3 reshape.102
  50.8 1.3 collective-permute-start
  52.1 1.3 collective-permute-start.1
  53.7 0.3 fusion.16
  54.0 3.4 %collective-permute-done.1 = bf16[16,1,128]{2,1,0:T(2,128)(2,1)S(1)} collective-permute-done((bf16[16,1,128]{2,1,0:T(2,128)(2,1)S(1)}, bf16[16,1,128]{2,1,0:T(2,128)(2,1)S(1)}, u32[]{:S(2)}, u32[]{:S(2)}) %collective-permute-start.1) | collective-permute-done | bytes 4128 | tf_op jit(solution)/shard_map/ppermute | solution.py:23
  57.4 0.4 multiply_reduce_fusion
  57.8 80.7 %all-gather.3.cloned.1.call-done = bf16[2048,3072]{1,0:T(8,128)(2,1)} async-done(((bf16[64,3072]{1,0:T(8,128)(2,1)}), bf16[2048,3072]{1,0:T(8,128)(2,1)}) %all-gather.3.cloned.1.call-update) | async-done | bytes 12582928 | tf_op jit(solution)/shard_map/all_gather | solution.py:60
  138.5 6.5 %convolution_convert_fusion.1 = bf16[128,3072]{1,0:T(8,128)(2,1)S(1)} fusion(bf16[2048,3072]{1,0:T(8,128)(2,1)} %all-gather.3.cloned.1.call-done, f32[128,2048]{1,0:T(8,128)S(1)} %get-tuple-element.72, f32[2048]{0:T(1024)S(1)} %copy-done.4, f32[128]{0:T(128)S(1)} %add_rsqrt_fusion), kind=kOutput, calls=%fused_computation.19 | convolution fusion | flops 1611792384 | bytes 14426624 | tf_op jit(solution)/shard_map/dot_general | solution.py:58
  145.0 2.9 %collective-permute-start.2 = (bf16[128,2048]{1,0:T(8,128)(2,1)S(1)}, bf16[128,2048]{1,0:T(8,128)(2,1)S(1)}, u32[]{:S(2)}, u32[]{:S(2)}) collective-permute-start(bf16[128,2048]{1,0:T(8,128)(2,1)S(1)} %slice.47), channel_id=1, source_target_pairs={{0,16},{16,32},{32,48},{48,64},{64,80},{80,96},{96,112},{112,128},... | collective-permute-start | bytes 1572872 | tf_op jit(solution)/shard_map/ppermute | solution.py:31
  148.1 1.9 collective-permute-start.4
  150.1 4.0 %collective-permute-done.2 = bf16[128,2048]{1,0:T(8,128)(2,1)S(1)} collective-permute-done((bf16[128,2048]{1,0:T(8,128)(2,1)S(1)}, bf16[128,2048]{1,0:T(8,128)(2,1)S(1)}, u32[]{:S(2)}, u32[]{:S(2)}) %collective-permute-start.2) | collective-permute-done | bytes 524320 | tf_op jit(solution)/shard_map/ppermute | solution.py:31
  154.1 4.4 %collective-permute-start.3 = (bf16[128,2048]{1,0:T(8,128)(2,1)S(1)}, bf16[128,2048]{1,0:T(8,128)(2,1)S(1)}, u32[]{:S(2)}, u32[]{:S(2)}) collective-permute-start(bf16[128,2048]{1,0:T(8,128)(2,1)S(1)} %collective-permute-done.2), channel_id=1, source_target_pairs={{0,16},{16,32},{32,48},{48,64},{64,80},{80,96},{96,112},{112,128},... | collective-permute-start | bytes 1572872 | tf_op jit(solution)/shard_map/ppermute | solution.py:31
  158.6 3.1 %collective-permute-done.4 = bf16[128,2048]{1,0:T(8,128)(2,1)S(1)} collective-permute-done((bf16[128,2048]{1,0:T(8,128)(2,1)S(1)}, bf16[128,2048]{1,0:T(8,128)(2,1)S(1)}, u32[]{:S(2)}, u32[]{:S(2)}) %collective-permute-start.4) | collective-permute-done | bytes 524320 | tf_op jit(solution)/shard_map/ppermute | solution.py:31
  161.7 1.9 collective-permute-start.5
  163.6 0.9 collective-permute-done.3
  164.7 11.3 %collective-permute-done.5 = bf16[128,2048]{1,0:T(8,128)(2,1)S(1)} collective-permute-done((bf16[128,2048]{1,0:T(8,128)(2,1)S(1)}, bf16[128,2048]{1,0:T(8,128)(2,1)S(1)}, u32[]{:S(2)}, u32[]{:S(2)}) %collective-permute-start.5) | collective-permute-done | bytes 524320 | tf_op jit(solution)/shard_map/ppermute | solution.py:31
  176.1 0.7 slice_bitcast_fusion
  176.8 0.6 bitcast_bitcast_fusion
  177.4 0.3 copy-done.3
  177.7 6.6 %while.11 = (s32[]{:T(128)}, bf16[8,128,128]{2,1,0:T(8,128)(2,1)S(1)}, bf16[8,128,128]{2,1,0:T(8,128)(2,1)S(1)}, bf16[8,640,128]{2,1,0:T(8,128)(2,1)S(1)}, bf16[...) while((s32[]{:T(128)}, bf16[8,128,128]{2,1,0:T(8,128)(2,1)S(1)}, ...), condition=%wide.region_5.6_spmd.clone, body=%wide.region_2.5_spmd.clone.sunk | while | flops 42614528 | bytes 1381965 | solution.py:89
  177.7 0.3 fusion.44
  178.6 0.3 fusion.44
  179.1 0.3 fusion.46
  179.4 0.3 fusion.44
  180.2 0.3 fusion.44
  181.0 0.3 fusion.44
  181.9 0.3 fusion.44
  182.7 0.3 fusion.44
  183.5 0.3 fusion.44
  184.5 0.8 reshape.99
  (44 shorter events, 4.7 us)
Async XLA Ops:
  6.5 44.2 %copy-start.2 = (bf16[16,8,128]{2,1,0:T(8,128)(2,1)S(1)}, bf16[16,8,128]{2,1,0:T(8,128)(2,1)}, u32[]{:S(2)}) copy-start(bf16[16,8,128]{2,1,0:T(8,128)(2,1)} %param.8) | copy-start | bytes 98308
  6.5 46.9 %copy-start = (bf16[3,128,2048]{2,1,0:T(8,128)(2,1)S(1)}, bf16[3,128,2048]{2,1,0:T(8,128)(2,1)}, u32[]{:S(2)}) copy-start(bf16[3,128,2048]{2,1,0:T(8,128)(2,1)} %param.10) | copy-start | bytes 4718596
  6.5 132.0 %all-gather.3.cloned.1.call-start = ((), (), s32[]{:S(2)}) async-start(), calls=%async_computation | async-start | bytes 12976128 | tf_op jit(solution)/shard_map/all_gather | solution.py:60
  49.4 4.3 %copy-start.1 = (bf16[16,8,2048]{2,1,0:T(8,128)(2,1)S(1)}, bf16[16,8,2048]{2,1,0:T(8,128)(2,1)}, u32[]{:S(2)}) copy-start(bf16[16,8,2048]{2,1,0:T(8,128)(2,1)} %param.9) | copy-start | bytes 1572868
  50.8 2.9 %collective-permute-start = (bf16[16,1,128]{2,1,0:T(2,128)(2,1)S(1)}, bf16[16,1,128]{2,1,0:T(2,128)(2,1)S(1)}, u32[]{:S(2)}, u32[]{:S(2)}) collective-permute-start(bf16[16,1,128]{2,1,0:T(2,128)(2,1)S(1)} %get-tuple-element.70), channel_id=1, source_target_pairs={{0,1},{1,2},{2,3},{3,4},{4,5},{5,6},{6,7},{7,8},{8,9},{9,10},{10,1... | collective-permute-start | bytes 12296 | tf_op jit(solution)/shard_map/ppermute | solution.py:22
  52.1 5.3 %collective-permute-start.1 = (bf16[16,1,128]{2,1,0:T(2,128)(2,1)S(1)}, bf16[16,1,128]{2,1,0:T(2,128)(2,1)S(1)}, u32[]{:S(2)}, u32[]{:S(2)}) collective-permute-start(bf16[16,1,128]{2,1,0:T(2,128)(2,1)S(1)} %get-tuple-element.69), channel_id=1, source_target_pairs={{1,0},{2,1},{3,2},{4,3},{5,4},{6,5},{7,6},{8,7},{9,8},{10,9},{11,1... | collective-permute-start | bytes 12296 | tf_op jit(solution)/shard_map/ppermute | solution.py:23
  54.0 84.5 %copy-start.4 = (f32[2048]{0:T(1024)S(1)}, f32[2048]{0:T(1024)}, u32[]{:S(2)}) copy-start(f32[2048]{0:T(1024)} %param.11) | copy-start | bytes 24580
  138.5 9.4 %copy-start.5 = (s32[1,1,5]{2,1,0:T(1,128)S(1)}, s32[1,1,5]{2,1,0:T(1,128)}, u32[]{:S(2)}) copy-start(s32[1,1,5]{2,1,0:T(1,128)} %param.13) | copy-start | bytes 64
  145.0 9.0 %collective-permute-start.2 = (bf16[128,2048]{1,0:T(8,128)(2,1)S(1)}, bf16[128,2048]{1,0:T(8,128)(2,1)S(1)}, u32[]{:S(2)}, u32[]{:S(2)}) collective-permute-start(bf16[128,2048]{1,0:T(8,128)(2,1)S(1)} %slice.47), channel_id=1, source_target_pairs={{0,16},{16,32},{32,48},{48,64},{64,80},{80,96},{96,112},{112,128},... | collective-permute-start | bytes 1572872 | tf_op jit(solution)/shard_map/ppermute | solution.py:31
  148.1 13.5 %collective-permute-start.4 = (bf16[128,2048]{1,0:T(8,128)(2,1)S(1)}, bf16[128,2048]{1,0:T(8,128)(2,1)S(1)}, u32[]{:S(2)}, u32[]{:S(2)}) collective-permute-start(bf16[128,2048]{1,0:T(8,128)(2,1)S(1)} %slice.47), channel_id=1, source_target_pairs={{16,0},{32,16},{48,32},{64,48},{80,64},{96,80},{112,96},{128,112},... | collective-permute-start | bytes 1572872 | tf_op jit(solution)/shard_map/ppermute | solution.py:31
  154.1 10.5 %collective-permute-start.3 = (bf16[128,2048]{1,0:T(8,128)(2,1)S(1)}, bf16[128,2048]{1,0:T(8,128)(2,1)S(1)}, u32[]{:S(2)}, u32[]{:S(2)}) collective-permute-start(bf16[128,2048]{1,0:T(8,128)(2,1)S(1)} %collective-permute-done.2), channel_id=1, source_target_pairs={{0,16},{16,32},{32,48},{48,64},{64,80},{80,96},{96,112},{112,128},... | collective-permute-start | bytes 1572872 | tf_op jit(solution)/shard_map/ppermute | solution.py:31
  161.7 14.4 %collective-permute-start.5 = (bf16[128,2048]{1,0:T(8,128)(2,1)S(1)}, bf16[128,2048]{1,0:T(8,128)(2,1)S(1)}, u32[]{:S(2)}, u32[]{:S(2)}) collective-permute-start(bf16[128,2048]{1,0:T(8,128)(2,1)S(1)} %collective-permute-done.4), channel_id=1, source_target_pairs={{16,0},{32,16},{48,32},{64,48},{80,64},{96,80},{112,96},{128,112},... | collective-permute-start | bytes 1572872 | tf_op jit(solution)/shard_map/ppermute | solution.py:31
  176.8 1.0 copy-start.3
Sparse Core Ops, SparseCore 0:
  50.9 87.5 all-gather.2
where the time goes:
time: 192 us
  waiting for transfers between devices  103 us (54%)
  blocking collectives  42.6 us (22%)
  starting transfers between devices  13.7 us (7%)
  between operations  13.6 us (7%)
  matrix products  12.1 us (6%)
  local copies, waits for them, and re-layouts  4.61 us (2%)
    all_gather x1, waiting for transfers between devices, per_device(): lax.all_gather(columns, 'tm', axis=0, tiled=True)  80.7 us
    all_gather x1, blocking collectives, per_device(): columns = lax.all_gather(w_qkv, 'depth', axis=1, tiled=True)  42.6 us
    ppermute x4, waiting for transfers between devices, from_behind(): return lax.ppermute(value, axis, pairs)  19.3 us
    ppermute x4, starting transfers between devices, from_behind(): return lax.ppermute(value, axis, pairs)  11.1 us
    dot_general x1, matrix products, per_device(): jnp.dot(normed, lax.all_gather(columns, 'tm', axis=0, tiled=True), prefer...  6.45 us
  transfers between devices with their start and end apart: 7, of which 6 were waited for; matrix products, arithmetic and copies ran while one was open for 1% of the time, Pallas kernels for 0%

commit v1 on v0

v1 whole, which is shorter than its diff:
```python
import math

import jax
import jax.numpy as jnp
from jax import lax
from jax.experimental import pallas as pl
from jax.experimental.pallas import tpu as pltpu
from jax.sharding import PartitionSpec as P

HEADS = 8
HD = 128
BF = jnp.bfloat16
F32 = jnp.float32


def layer(raw, stream, conv, gain, w, mrow, out, pad, rleft, rright, emb, tok, wy, wp, wfull, acc,
          q, kv, masks, ctx_out, ctx_in, s_w, r_w, s_raw, r_raw, s_m, r_m, s_d, r_d, s_t, r_t,
          s_z, r_z, s_kv, r_kv, s_c, r_c):
    tm, depth = lax.axis_index("tm"), lax.axis_index("depth")
    z, g = tm // 4, tm % 4
    x, yh = depth // 4, depth % 4
    up, down = (depth + 1) % 16, (depth + 15) % 16
    zr, zl = (z + 1) % 8, (z + 7) % 8

    def send(src, dst, s, r, to):
        return pltpu.make_async_remote_copy(
            src_ref=src, dst_ref=dst, send_sem=s, recv_sem=r, device_id=to,
            device_id_type=pl.DeviceIdType.MESH)

    barrier = pltpu.get_barrier_semaphore()

    def greet(a, b):
        pl.semaphore_signal(barrier, inc=1, device_id=(a, b), device_id_type=pl.DeviceIdType.MESH)

    for k in range(1, 4):
        greet(tm, 4 * x + (yh + k) % 4)
    greet(tm, up)
    greet(tm, down)
    greet(4 * zr + g, depth)
    greet(4 * zl + g, depth)
    for a in range(4):
        for b in range(4):
            if a or b:
                greet(4 * z + (g + a) % 4, 4 * ((x + b) % 4) + yh)
    pl.semaphore_wait(barrier, 22)

    w_copies = [send(w, wy.at[yh], s_w.at[k - 1], r_w.at[k - 1], (tm, 4 * x + (yh + k) % 4))
                for k in range(1, 4)]
    for c in w_copies:
        c.start()
    raw_up = send(raw, rleft, s_raw.at[0], r_raw.at[0], (tm, up))
    raw_down = send(raw, rright, s_raw.at[1], r_raw.at[1], (tm, down))
    raw_up.start()
    raw_down.start()
    m_copies = [send(mrow, masks.at[g], s_m.at[k - 1], r_m.at[k - 1], (4 * z + (g + k) % 4, depth))
                for k in range(1, 4)]
    for c in m_copies:
        c.start()
    masks[g] = mrow[...]
    wy[yh] = w[...]

    for c in w_copies:
        c.wait()
    parts = [wy[i].astype(F32) for i in range(4)]
    wp[0] = jnp.concatenate([parts[0], parts[1][:, :64]], axis=1).astype(BF)
    wp[1] = jnp.concatenate([parts[1][:, 64:], parts[2][:, :128]], axis=1).astype(BF)
    wp[2] = jnp.concatenate([parts[2][:, 128:], parts[3]], axis=1).astype(BF)
    rows = pl.ds(pl.multiple_of(g * 64, 64), 64)

    def direct(j, k):
        pair = 3 * x + j
        return send(wp.at[j], wfull.at[z, pair // 4, rows], s_d.at[j, k], r_d.at[pair // 4, g],
                    (4 * z + pair % 4, 4 * ((x + k) % 4) + yh))

    def kept(j):
        pair = 3 * x + j
        return pltpu.make_async_copy(wp.at[j], wfull.at[z, pair // 4, rows], r_d.at[pair // 4, g])

    for j in range(3):
        for k in range(1, 4):
            direct(j, k).start()

        @pl.when((3 * x + j) % 4 != g)
        def _():
            direct(j, 0).start()

        @pl.when((3 * x + j) % 4 == g)
        def _():
            kept(j).start()

    raw_up.wait()
    raw_down.wait()
    pad[:, 1:9, :] = raw[...].astype(F32)
    pad[:, 0:1, :] = jnp.where(depth == 0, 0.0, rleft[:, 7:8, :].astype(F32))
    pad[:, 9:10, :] = jnp.where(depth == 15, 0.0, rright[:, 0:1, :].astype(F32))
    windows = [pad[:, j:j + 8, :].reshape(128, 128).astype(BF) for j in range(3)]
    squares = jnp.zeros((128, 1), F32)
    for n in range(4):
        cols = slice(512 * n, 512 * n + 512)
        e = stream[:, cols].astype(F32)
        for j in range(3):
            e = e + jnp.dot(windows[j], conv[j, :, cols], preferred_element_type=F32)
        emb[:, cols] = e
        squares = squares + jnp.sum(e * e, axis=-1, keepdims=True)
    inv = lax.rsqrt(squares * (1.0 / 2048) + 1e-05)
    tok[g] = (emb[...] * inv * gain[...]).astype(BF)
    partner = g + 1 - 2 * (g % 2)
    across = (g + 2) % 4
    t_across = send(tok.at[g], tok.at[g], s_t.at[0], r_t.at[0], (4 * z + across, depth))
    t_partner = send(tok.at[g], tok.at[g], s_t.at[1], r_t.at[1], (4 * z + partner, depth))
    t_relay = send(tok.at[across], tok.at[across], s_t.at[2], r_t.at[2], (4 * z + partner, depth))
    t_across.start()
    t_partner.start()

    for kind in range(3):
        for i in range(4):
            pltpu.make_async_copy(wp.at[0], wfull.at[z, kind, pl.ds(64 * i, 64)], r_d.at[kind, i]).wait()

    def half(c, h):
        return wfull.at[c, :, pl.ds(128 * h, 128)]

    def ring(way, step, h):
        c = (z + 8 - step) % 8 if way == 0 else (z + step) % 8
        i = 2 * step + (h if step < 3 else 0)
        return send(half(c, h), half(c, h), s_z.at[way, i], r_z.at[way, i],
                    (4 * (zr if way == 0 else zl) + g, depth))

    def halves(way, step):
        return (0, 1) if step < 3 else (way,)

    def multiply(c, first):
        cols = pl.ds(pl.multiple_of(c * 256, 256), 256)

        def one(kind, carry):
            product = jnp.dot(tok[:, :, cols].reshape(512, 256), wfull[c, kind],
                              preferred_element_type=F32)
            acc[kind] = product if first else acc[kind] + product
            return carry

        lax.fori_loop(0, 3, one, 0)

    for h in (0, 1):
        for way in (0, 1):
            ring(way, 0, h).start()
    t_across.wait_recv()
    t_relay.start()
    t_partner.wait_recv()
    t_relay.wait_recv()
    multiply(z, True)
    for step in range(4):
        for h in (0, 1):
            for way in (0, 1):
                if h in halves(way, step):
                    ring(way, step, h).wait_recv()
                    if step < 3 and h in halves(way, step + 1):
                        ring(way, step + 1, h).start()
        multiply((z + 7 - step) % 8, False)
        if step < 3:
            multiply((z + 1 + step) % 8, False)

    for b in range(4):
        kv[2 + b, :, :256] = acc[1, 128 * b:128 * b + 128].astype(BF)
        kv[2 + b, :, 256:] = acc[2, 128 * b:128 * b + 128].astype(BF)
    kv_ahead = send(kv.at[pl.ds(4, 2)], kv.at[pl.ds(0, 2)], s_kv.at[0], r_kv.at[0], (4 * zr + g, depth))
    kv_back = send(kv.at[pl.ds(2, 2)], kv.at[pl.ds(6, 2)], s_kv.at[1], r_kv.at[1], (4 * zl + g, depth))
    kv_ahead.start()
    kv_back.start()
    for b in range(4):
        q[b] = acc[0, 128 * b:128 * b + 128].astype(BF)
    for c in m_copies:
        c.wait()
    kv_ahead.wait()
    kv_back.wait()

    def attend(b):
        allowed = masks[b][0:1, :] > 0.5
        halves_out = []
        for h in range(2):
            keys = kv[pl.ds(b, 5), :, 128 * h:128 * h + 128].reshape(640, 128)
            values = kv[pl.ds(b, 5), :, 256 + 128 * h:384 + 128 * h].reshape(640, 128)
            query = q[b, :, 128 * h:128 * h + 128]
            scores = lax.dot_general(query, keys, (((1,), (1,)), ((), ())),
                                     preferred_element_type=F32) * (1.0 / math.sqrt(HD))
            scores = jnp.where(allowed, scores, -1e30)
            powers = jnp.exp(scores - jnp.max(scores, axis=-1, keepdims=True))
            weights = (powers / jnp.sum(powers, axis=-1, keepdims=True)).astype(BF)
            halves_out.append(jnp.dot(weights, values, preferred_element_type=F32).astype(BF))
        return halves_out

    def give(k):
        return send(ctx_out.at[k - 1], ctx_in.at[g], s_c.at[k - 1], r_c.at[k - 1],
                    (4 * z + (g + k) % 4, depth))

    for k in (2, 3, 1, 0):
        pieces = attend((g + k) % 4)
        for h in range(2):
            if k:
                ctx_out[k - 1, :, 128 * h:128 * h + 128] = pieces[h]
            else:
                ctx_in[g, :, 128 * h:128 * h + 128] = pieces[h]
        if k:
            give(k).start()

    for j in range(3):
        for k in range(1, 4):
            direct(j, k).wait_send()

        @pl.when((3 * x + j) % 4 != g)
        def _():
            direct(j, 0).wait_send()

    t_across.wait_send()
    t_partner.wait_send()
    t_relay.wait_send()
    for way in (0, 1):
        for step in range(4):
            for h in halves(way, step):
                ring(way, step, h).wait_send()
    for k in (2, 3, 1):
        give(k).wait()
    for i in range(4):
        out[:, 256 * i:256 * i + 256] = ctx_in[i]


def per_device(raw, stream, conv_w, gain, w_qkv, mask):
    mrow = jnp.broadcast_to(jnp.repeat(mask.reshape(1, 5).astype(F32), 128, axis=1), (8, 640))
    vmem = pltpu.VMEM
    dma = pltpu.SemaphoreType.DMA
    context = pl.pallas_call(
        layer,
        out_shape=jax.ShapeDtypeStruct((128, 1024), BF),
        in_specs=[pl.BlockSpec(memory_space=pltpu.VMEM)] * 6,
        out_specs=pl.BlockSpec(memory_space=pltpu.VMEM),
        scratch_shapes=[
            vmem((16, 16, 128), F32), vmem((16, 8, 128), BF), vmem((16, 8, 128), BF),
            vmem((128, 2048), F32), vmem((4, 128, 2048), BF), vmem((4, 64, 192), BF),
            vmem((3, 64, 256), BF), vmem((8, 3, 256, 256), BF), vmem((3, 512, 256), F32),
            vmem((4, 128, 256), BF), vmem((8, 128, 512), BF), vmem((4, 8, 640), F32),
            vmem((3, 128, 256), BF), vmem((4, 128, 256), BF),
            dma((3,)), dma((3,)), dma((2,)), dma((2,)), dma((3,)), dma((3,)),
            dma((3, 4)), dma((3, 4)), dma((3,)), dma((3,)), dma((2, 7)), dma((2, 7)),
            dma((2,)), dma((2,)), dma((3,)), dma((3,)),
        ],
        compiler_params=pltpu.CompilerParams(
            collective_id=0, has_side_effects=True, vmem_limit_bytes=48 * 1024 * 1024),
    )(raw, stream.reshape(128, 2048), conv_w, gain.reshape(1, 2048), w_qkv, mrow)
    return context.reshape(16, 8, 1024)


def solution(mesh):
    in_specs = (P("tm", "depth", None), P("tm", "depth", None), P(), P(), P("tm", "depth"),
                P("depth", "tm", None))
    return jax.shard_map(per_device, mesh=mesh, in_specs=in_specs,
                         out_specs=P("tm", "depth", None), check_vma=False)
```

time: 192 us -> 89.4 us (0.47)
  waiting for transfers between devices: 103 us -> 0 us
  Pallas kernels: 0 us -> 82.9 us
  blocking collectives: 42.6 us -> 0 us
  starting transfers between devices: 13.7 us -> 0 us
  between operations: 13.6 us -> 0.02 us
  matrix products: 12.1 us -> 0 us
    pallas_call x0 -> x1, Pallas kernels: none -> 82.9 us  [per_device(): pl.pallas_call(layer, out_shape=jax.ShapeDtypeStruct((128, 1024), BF), in...]
    all_gather x1 -> x0, waiting for transfers between devices: 80.7 us -> none  [per_device(): lax.all_gather(columns, 'tm', axis=0, tiled=True)]
    all_gather x1 -> x0, blocking collectives: 42.6 us -> none  [per_device(): columns = lax.all_gather(w_qkv, 'depth', axis=1, tiled=True)]
    ppermute x6 -> x0, waiting for transfers between devices: 22.7 us -> none  [the longest x4 19.3 us: from_behind(): return lax.ppermute(value, axis, pairs)]
    ppermute x6 -> x0, starting transfers between devices: 13.7 us -> none  [the longest x4 11.1 us: from_behind(): return lax.ppermute(value, axis, pairs)]
    dot_general x20 -> x0, matrix products: 12.1 us -> none  [the longest x1 6.45 us: per_device(): jnp.dot(normed, lax.all_gather(columns, 'tm', axis=0, tiled=True), prefer...]
    unnamed x18 -> x11, local copies, waits for them, and re-layouts: 2.5 us -> 5.36 us
  transfers between devices with their start and end apart: 7 -> 0, of which waited for: 6 -> 0; matrix products, arithmetic and copies ran while one was open for 1% -> 0% of each run, Pallas kernels for 0% -> 0%
where the time goes in v1:
time: 89.4 us; the launch traced here: 89 us
  Pallas kernels  82.9 us (93%)
  local copies, waits for them, and re-layouts  5.44 us (6%)
    pallas_call x1, Pallas kernels, per_device(): pl.pallas_call(layer, out_shape=jax.ShapeDtypeStruct((128, 1024), BF), in...  82.9 us
    unnamed x11, local copies, waits for them, and re-layouts  5.36 us

profile of v1, /device:TPU:1, one launch (start us, length us, event | category | flops | bytes accessed | tf_op | source)
XLA Modules:
  0.0 89.0 jit_solution(2091094998163534562)
XLA Ops:
  0.0 0.7 convert_bitcast_fusion
  0.7 0.1 broadcast_bitcast_fusion
  0.7 0.0 copy-start
  0.7 1.4 %copy-done = bf16[3,128,2048]{2,1,0:T(8,128)(2,1)S(1)} copy-done((bf16[3,128,2048]{2,1,0:T(8,128)(2,1)S(1)}, bf16[3,128,2048]{2,1,0:T(8,128)(2,1)}, u32[]{:S(2)}) %copy-start) | copy-done | bytes 1572888
  2.1 0.0 copy-start.1
  2.1 1.0 %copy-done.1 = bf16[16,8,2048]{2,1,0:T(8,128)(2,1)S(1)} copy-done((bf16[16,8,2048]{2,1,0:T(8,128)(2,1)S(1)}, bf16[16,8,2048]{2,1,0:T(8,128)(2,1)}, u32[]{:S(2)}) %copy-start.1) | copy-done | bytes 524312
  3.2 0.0 copy-start.2
  3.2 0.8 copy-done.2
  3.9 0.0 copy-start.3
  3.9 0.8 copy-done.3
  4.7 0.0 copy-start.4
  4.7 0.7 copy-done.4
  5.4 82.9 %shard_map.64 = bf16[128,1024]{1,0:T(8,128)(2,1)S(1)} custom-call(bf16[16,8,128]{2,1,0:T(8,128)(2,1)S(1)} %copy-done.2, bf16[128,2048]{1,0:T(8,128)(2,1)S(1)} %bitcast.8, bf16[3,128,2048]{2,1,0:T(8,128)(2,1)S(1)} %copy-done, f32[1,2048]{1,0:T(1,128)S(1)} %bitcast.9, bf16[64,192]{1,0:T(8,128)(2,1)S(1)} %copy-done.3, f32[8,640]{1,0:T(8,128)S(1)} %broadcast_in_dim.12.mrow), custom_call_target="tpu_custom_call" | custom-call | tf_op jit(solution)/shard_map/pallas_call | solution.py:229
  88.3 0.7 copy.8
  (1 shorter events, 0.0 us)
Async XLA Ops:
  0.7 1.4 %copy-start = (bf16[3,128,2048]{2,1,0:T(8,128)(2,1)S(1)}, bf16[3,128,2048]{2,1,0:T(8,128)(2,1)}, u32[]{:S(2)}) copy-start(bf16[3,128,2048]{2,1,0:T(8,128)(2,1)} %conv.1) | copy-start | bytes 4718596
  2.1 1.0 %copy-start.1 = (bf16[16,8,2048]{2,1,0:T(8,128)(2,1)S(1)}, bf16[16,8,2048]{2,1,0:T(8,128)(2,1)}, u32[]{:S(2)}) copy-start(bf16[16,8,2048]{2,1,0:T(8,128)(2,1)} %param.7) | copy-start | bytes 1572868
  3.2 0.8 copy-start.2
  3.9 0.8 copy-start.3
  4.7 0.7 copy-start.4

commit v2 on v1

--- a/solution.py
+++ b/solution.py
@@ -13,14 +13,21 @@
 F32 = jnp.float32
 
 
-def layer(raw, stream, conv, gain, w, mrow, out, pad, rleft, rright, emb, tok, wy, wp, wfull, acc,
-          q, kv, masks, ctx_out, ctx_in, s_w, r_w, s_raw, r_raw, s_m, r_m, s_d, r_d, s_t, r_t,
-          s_z, r_z, s_kv, r_kv, s_c, r_c):
+def layer(raw_h, stream_h, conv_h, gain_h, w_h, mrow, out, raw, stream, conv, gain, pad, rleft, rright,
+          emb, tok, wy, wp, wfull, acc, q, kv, masks, ctx_out, ctx_in, s_in, s_w, r_w, s_raw, r_raw,
+          s_m, r_m, s_d, r_d, s_e, r_e, s_t, r_t, s_z, r_z, s_b, r_b, s_x, r_x, s_f, r_f, s_kv, r_kv,
+          s_c, r_c):
     tm, depth = lax.axis_index("tm"), lax.axis_index("depth")
     z, g = tm // 4, tm % 4
     x, yh = depth // 4, depth % 4
     up, down = (depth + 1) % 16, (depth + 15) % 16
     zr, zl = (z + 1) % 8, (z + 7) % 8
+    xr, xl = (x + 1) % 4, (x + 3) % 4
+
+    loads = [pltpu.make_async_copy(a, b, s_in.at[i]) for i, (a, b) in enumerate(
+        ((w_h, wy.at[yh]), (raw_h, raw), (conv_h, conv), (stream_h, stream), (gain_h, gain)))]
+    for c in loads:
+        c.start()
 
     def send(src, dst, s, r, to):
         return pltpu.make_async_remote_copy(
@@ -44,12 +51,12 @@
                 greet(4 * z + (g + a) % 4, 4 * ((x + b) % 4) + yh)
     pl.semaphore_wait(barrier, 22)
 
-    w_copies = [send(w, wy.at[yh], s_w.at[k - 1], r_w.at[k - 1], (tm, 4 * x + (yh + k) % 4))
+    w_copies = [send(w_h, wy.at[yh], s_w.at[k - 1], r_w.at[k - 1], (tm, 4 * x + (yh + k) % 4))
                 for k in range(1, 4)]
     for c in w_copies:
         c.start()
-    raw_up = send(raw, rleft, s_raw.at[0], r_raw.at[0], (tm, up))
-    raw_down = send(raw, rright, s_raw.at[1], r_raw.at[1], (tm, down))
+    raw_up = send(raw_h, rleft, s_raw.at[0], r_raw.at[0], (tm, up))
+    raw_down = send(raw_h, rright, s_raw.at[1], r_raw.at[1], (tm, down))
     raw_up.start()
     raw_down.start()
     m_copies = [send(mrow, masks.at[g], s_m.at[k - 1], r_m.at[k - 1], (4 * z + (g + k) % 4, depth))
@@ -57,8 +64,8 @@
     for c in m_copies:
         c.start()
     masks[g] = mrow[...]
-    wy[yh] = w[...]
-
+
+    loads[0].wait()
     for c in w_copies:
         c.wait()
     parts = [wy[i].astype(F32) for i in range(4)]
@@ -67,27 +74,57 @@
     wp[2] = jnp.concatenate([parts[2][:, 128:], parts[3]], axis=1).astype(BF)
     rows = pl.ds(pl.multiple_of(g * 64, 64), 64)
 
-    def direct(j, k):
+    def to_all(j, k):
         pair = 3 * x + j
-        return send(wp.at[j], wfull.at[z, pair // 4, rows], s_d.at[j, k], r_d.at[pair // 4, g],
+        return send(wp.at[j], wfull.at[z, 0, rows], s_d.at[j, k], r_d.at[g],
                     (4 * z + pair % 4, 4 * ((x + k) % 4) + yh))
 
-    def kept(j):
+    def to_one(j):
         pair = 3 * x + j
-        return pltpu.make_async_copy(wp.at[j], wfull.at[z, pair // 4, rows], r_d.at[pair // 4, g])
+        return send(wp.at[j], wfull.at[z, pair // 4, rows], s_e.at[j], r_e.at[pair // 4],
+                    (4 * z + pair % 4, 4 * g + yh))
+
+    def keep_query(j):
+        return pltpu.make_async_copy(wp.at[j], wfull.at[z, 0, rows], r_d.at[g])
+
+    def keep_other(j):
+        pair = 3 * x + j
+        return pltpu.make_async_copy(wp.at[j], wfull.at[z, pair // 4, rows], r_e.at[pair // 4])
+
+    def direct(j, act, stay):
+        pair = 3 * x + j
+        mine = pair % 4 == g
+
+        @pl.when(pair < 4)
+        def _():
+            for k in range(1, 4):
+                act(to_all(j, k))
+
+            @pl.when(mine)
+            def _():
+                stay(keep_query(j))
+
+            @pl.when(jnp.logical_not(mine))
+            def _():
+                act(to_all(j, 0))
+
+        @pl.when(pair >= 4)
+        def _():
+            own = jnp.logical_and(mine, x == g)
+
+            @pl.when(own)
+            def _():
+                stay(keep_other(j))
+
+            @pl.when(jnp.logical_not(own))
+            def _():
+                act(to_one(j))
 
     for j in range(3):
-        for k in range(1, 4):
-            direct(j, k).start()
-
-        @pl.when((3 * x + j) % 4 != g)
-        def _():
-            direct(j, 0).start()
-
-        @pl.when((3 * x + j) % 4 == g)
-        def _():
-            kept(j).start()
-
+        direct(j, lambda c: c.start(), lambda c: c.start())
+
+    for c in loads[1:]:
+        c.wait()
     raw_up.wait()
     raw_down.wait()
     pad[:, 1:9, :] = raw[...].astype(F32)
@@ -112,12 +149,8 @@
     t_across.start()
     t_partner.start()
 
-    for kind in range(3):
-        for i in range(4):
-            pltpu.make_async_copy(wp.at[0], wfull.at[z, kind, pl.ds(64 * i, 64)], r_d.at[kind, i]).wait()
-
     def half(c, h):
-        return wfull.at[c, :, pl.ds(128 * h, 128)]
+        return wfull.at[c, 0, pl.ds(128 * h, 128)]
 
     def ring(way, step, h):
         c = (z + 8 - step) % 8 if way == 0 else (z + step) % 8
@@ -128,35 +161,94 @@
     def halves(way, step):
         return (0, 1) if step < 3 else (way,)
 
-    def multiply(c, first):
+    def quarter(c, kinds, at):
+        return wfull.at[c, kinds, pl.ds(pl.multiple_of(64 * at, 64), 64)]
+
+    both = pl.ds(1, 2)
+
+    def narrow(way, step):
+        c = (z + 8 - step) % 8 if way == 0 else (z + step) % 8
+        part = quarter(c, both if step < 3 else pl.ds(1 + way, 1), x)
+        return send(part, part, s_b.at[way, step], r_b.at[way, step],
+                    (4 * (zr if way == 0 else zl) + g, depth))
+
+    def chunk_of(i):
+        return (z + 8 - i) % 8 if i < 4 else (z + i - 3) % 8
+
+    def spread(way, i):
+        part = quarter(chunk_of(i), both, x)
+        return send(part, part, s_x.at[way, i], r_x.at[way, i], (tm, 4 * (xr if way == 0 else xl) + yh))
+
+    def pass_on(way, i):
+        part = quarter(chunk_of(i), pl.ds(1 + way, 1), xl if way == 0 else xr)
+        return send(part, part, s_f.at[way, i], r_f.at[way, i], (tm, 4 * (xr if way == 0 else xl) + yh))
+
+    def relay(i):
+        for way in (0, 1):
+            spread(way, i).wait_recv()
+            pass_on(way, i).start()
+
+    def multiply(i):
+        c = chunk_of(i)
         cols = pl.ds(pl.multiple_of(c * 256, 256), 256)
+        for way in (0, 1):
+            pass_on(way, i).wait_recv()
 
         def one(kind, carry):
             product = jnp.dot(tok[:, :, cols].reshape(512, 256), wfull[c, kind],
                               preferred_element_type=F32)
-            acc[kind] = product if first else acc[kind] + product
+            acc[kind] = acc[kind] + product if i else product
             return carry
 
         lax.fori_loop(0, 3, one, 0)
 
+    for kind in (1, 2):
+        pltpu.make_async_copy(wp.at[0], quarter(z, kind, x), r_e.at[kind]).wait()
+    for way in (0, 1):
+        narrow(way, 0).start()
+    for way in (0, 1):
+        spread(way, 0).start()
+    for i in range(4):
+        pltpu.make_async_copy(wp.at[0], wfull.at[z, 0, pl.ds(64 * i, 64)], r_d.at[i]).wait()
     for h in (0, 1):
         for way in (0, 1):
             ring(way, 0, h).start()
-    t_across.wait_recv()
-    t_relay.start()
-    t_partner.wait_recv()
-    t_relay.wait_recv()
-    multiply(z, True)
     for step in range(4):
+        for way in (0, 1):
+            narrow(way, step).wait_recv()
+            if step < 3:
+                narrow(way, step + 1).start()
+                for to in (0, 1):
+                    spread(to, (1 if way == 0 else 4) + step).start()
+        if step == 3:
+            for to in (0, 1):
+                spread(to, 7).start()
         for h in (0, 1):
             for way in (0, 1):
                 if h in halves(way, step):
                     ring(way, step, h).wait_recv()
                     if step < 3 and h in halves(way, step + 1):
                         ring(way, step + 1, h).start()
-        multiply((z + 7 - step) % 8, False)
-        if step < 3:
-            multiply((z + 1 + step) % 8, False)
+        if step == 0:
+            relay(0)
+        else:
+            relay(step)
+            relay(step + 3)
+        if step == 1:
+            t_across.wait_recv()
+            t_relay.start()
+        if step == 2:
+            t_partner.wait_recv()
+            t_relay.wait_recv()
+            multiply(0)
+            multiply(1)
+            multiply(4)
+    multiply(2)
+    multiply(5)
+    relay(7)
+    multiply(3)
+    multiply(6)
+    multiply(7)
 
     for b in range(4):
         kv[2 + b, :, :256] = acc[1, 128 * b:128 * b + 128].astype(BF)
@@ -202,13 +294,7 @@
             give(k).start()
 
     for j in range(3):
-        for k in range(1, 4):
-            direct(j, k).wait_send()
-
-        @pl.when((3 * x + j) % 4 != g)
-        def _():
-            direct(j, 0).wait_send()
-
+        direct(j, lambda c: c.wait_send(), lambda c: None)
     t_across.wait_send()
     t_partner.wait_send()
     t_relay.wait_send()
@@ -216,6 +302,10 @@
         for step in range(4):
             for h in halves(way, step):
                 ring(way, step, h).wait_send()
+            narrow(way, step).wait_send()
+        for i in range(8):
+            spread(way, i).wait_send()
+            pass_on(way, i).wait_send()
     for k in (2, 3, 1):
         give(k).wait()
     for i in range(4):
@@ -229,20 +319,22 @@
     context = pl.pallas_call(
         layer,
         out_shape=jax.ShapeDtypeStruct((128, 1024), BF),
-        in_specs=[pl.BlockSpec(memory_space=pltpu.VMEM)] * 6,
+        in_specs=[pl.BlockSpec(memory_space=pl.ANY)] * 5 + [pl.BlockSpec(memory_space=pltpu.VMEM)],
         out_specs=pl.BlockSpec(memory_space=pltpu.VMEM),
         scratch_shapes=[
+            vmem((16, 8, 128), BF), vmem((128, 2048), BF), vmem((3, 128, 2048), BF), vmem((1, 2048), F32),
             vmem((16, 16, 128), F32), vmem((16, 8, 128), BF), vmem((16, 8, 128), BF),
             vmem((128, 2048), F32), vmem((4, 128, 2048), BF), vmem((4, 64, 192), BF),
             vmem((3, 64, 256), BF), vmem((8, 3, 256, 256), BF), vmem((3, 512, 256), F32),
             vmem((4, 128, 256), BF), vmem((8, 128, 512), BF), vmem((4, 8, 640), F32),
             vmem((3, 128, 256), BF), vmem((4, 128, 256), BF),
-            dma((3,)), dma((3,)), dma((2,)), dma((2,)), dma((3,)), dma((3,)),
-            dma((3, 4)), dma((3, 4)), dma((3,)), dma((3,)), dma((2, 7)), dma((2, 7)),
-            dma((2,)), dma((2,)), dma((3,)), dma((3,)),
+            dma((5,)), dma((3,)), dma((3,)), dma((2,)), dma((2,)), dma((3,)), dma((3,)),
+            dma((3, 4)), dma((4,)), dma((3,)), dma((3,)), dma((3,)), dma((3,)),
+            dma((2, 7)), dma((2, 7)), dma((2, 4)), dma((2, 4)), dma((2, 8)), dma((2, 8)),
+            dma((2, 8)), dma((2, 8)), dma((2,)), dma((2,)), dma((3,)), dma((3,)),
         ],
         compiler_params=pltpu.CompilerParams(
-            collective_id=0, has_side_effects=True, vmem_limit_bytes=48 * 1024 * 1024),
+            collective_id=0, has_side_effects=True, vmem_limit_bytes=66_000_000),
     )(raw, stream.reshape(128, 2048), conv_w, gain.reshape(1, 2048), w_qkv, mrow)
     return context.reshape(16, 8, 1024)
 

time: 89.4 us -> 69.9 us (0.78)
  Pallas kernels: 82.9 us -> 66.7 us
  local copies, waits for them, and re-layouts: 5.44 us -> 2.35 us
    pallas_call x1, Pallas kernels: 82.9 us -> 66.7 us  [per_device(): pl.pallas_call(layer, out_shape=jax.ShapeDtypeStruct((128, 1024), BF), in...]
    unnamed x11 -> x1, local copies, waits for them, and re-layouts: 5.36 us -> 1.67 us
where the time goes in v2:
time: 69.9 us; the launch traced here: 69.7 us
  Pallas kernels  66.7 us (95%)
  local copies, waits for them, and re-layouts  2.35 us (3%)
    pallas_call x1, Pallas kernels, per_device(): pl.pallas_call(layer, out_shape=jax.ShapeDtypeStruct((128, 1024), BF), in...  66.7 us
    unnamed x1, local copies, waits for them, and re-layouts  1.67 us

profile of v2, /device:TPU:1, one launch (start us, length us, event | category | flops | bytes accessed | tf_op | source)
XLA Modules:
  0.0 69.7 jit_solution(11656766760535509903)
XLA Ops:
  0.0 0.7 convert_bitcast_fusion
  0.7 0.1 broadcast_bitcast_fusion
  0.7 0.6 broadcast_in_dim.12.mrow
  1.3 66.7 %shard_map.64 = bf16[128,1024]{1,0:T(8,128)(2,1)} custom-call(bf16[16,8,128]{2,1,0:T(8,128)(2,1)} %raw_h.1, bf16[128,2048]{1,0:T(8,128)(2,1)} %bitcast.8, bf16[3,128,2048]{2,1,0:T(8,128)(2,1)} %conv_h.1, f32[1,2048]{1,0:T(1,128)} %bitcast.9, bf16[64,192]{1,0:T(8,128)(2,1)} %w_h.1, f32[8,640]{1,0:T(8,128)} %broadcast_in_dim.12.mrow), custom_call_target="tpu_custom_call" | custom-call | tf_op jit(solution)/shard_map/pallas_call | solution.py:319
  68.1 1.7 %copy.8 = bf16[16,8,1024]{2,1,0:T(8,128)(2,1)} copy(bf16[16,8,1024]{2,1,0:T(8,128)(2,1)} %bitcast.7) | data formatting | bytes 524288

commit v3 on v2

--- a/solution.py
+++ b/solution.py
@@ -13,7 +13,7 @@
 F32 = jnp.float32
 
 
-def layer(raw_h, stream_h, conv_h, gain_h, w_h, mrow, out, raw, stream, conv, gain, pad, rleft, rright,
+def layer(raw_h, stream_h, conv_h, gain_h, w_h, mask_h, out, raw, stream, conv, gain, pad, rleft, rright,
           emb, tok, wy, wp, wfull, acc, q, kv, masks, ctx_out, ctx_in, s_in, s_w, r_w, s_raw, r_raw,
           s_m, r_m, s_d, r_d, s_e, r_e, s_t, r_t, s_z, r_z, s_b, r_b, s_x, r_x, s_f, r_f, s_kv, r_kv,
           s_c, r_c):
@@ -25,7 +25,8 @@
     xr, xl = (x + 1) % 4, (x + 3) % 4
 
     loads = [pltpu.make_async_copy(a, b, s_in.at[i]) for i, (a, b) in enumerate(
-        ((w_h, wy.at[yh]), (raw_h, raw), (conv_h, conv), (stream_h, stream), (gain_h, gain)))]
+        ((w_h, wy.at[yh]), (raw_h, raw), (conv_h, conv), (stream_h, stream), (gain_h, gain),
+         (mask_h, masks.at[g])))]
     for c in loads:
         c.start()
 
@@ -59,11 +60,10 @@
     raw_down = send(raw_h, rright, s_raw.at[1], r_raw.at[1], (tm, down))
     raw_up.start()
     raw_down.start()
-    m_copies = [send(mrow, masks.at[g], s_m.at[k - 1], r_m.at[k - 1], (4 * z + (g + k) % 4, depth))
+    m_copies = [send(mask_h, masks.at[g], s_m.at[k - 1], r_m.at[k - 1], (4 * z + (g + k) % 4, depth))
                 for k in range(1, 4)]
     for c in m_copies:
         c.start()
-    masks[g] = mrow[...]
 
     loads[0].wait()
     for c in w_copies:
@@ -234,20 +234,15 @@
         else:
             relay(step)
             relay(step + 3)
-        if step == 1:
+        if step == 2:
             t_across.wait_recv()
             t_relay.start()
-        if step == 2:
             t_partner.wait_recv()
-            t_relay.wait_recv()
-            multiply(0)
-            multiply(1)
-            multiply(4)
-    multiply(2)
-    multiply(5)
-    relay(7)
-    multiply(3)
-    multiply(6)
+    t_relay.wait_recv()
+    for i in (0, 1, 4, 2, 5, 3, 6):
+        multiply(i)
+        if i == 1:
+            relay(7)
     multiply(7)
 
     for b in range(4):
@@ -265,7 +260,8 @@
     kv_back.wait()
 
     def attend(b):
-        allowed = masks[b][0:1, :] > 0.5
+        row = masks[b]
+        allowed = jnp.concatenate([jnp.broadcast_to(row[:, e:e + 1], (1, 128)) for e in range(5)], axis=1) > 0
         halves_out = []
         for h in range(2):
             keys = kv[pl.ds(b, 5), :, 128 * h:128 * h + 128].reshape(640, 128)
@@ -313,29 +309,29 @@
 
 
 def per_device(raw, stream, conv_w, gain, w_qkv, mask):
-    mrow = jnp.broadcast_to(jnp.repeat(mask.reshape(1, 5).astype(F32), 128, axis=1), (8, 640))
     vmem = pltpu.VMEM
     dma = pltpu.SemaphoreType.DMA
     context = pl.pallas_call(
         layer,
         out_shape=jax.ShapeDtypeStruct((128, 1024), BF),
-        in_specs=[pl.BlockSpec(memory_space=pl.ANY)] * 5 + [pl.BlockSpec(memory_space=pltpu.VMEM)],
+        in_specs=[pl.BlockSpec(memory_space=pltpu.HBM)] * 6,
         out_specs=pl.BlockSpec(memory_space=pltpu.VMEM),
         scratch_shapes=[
             vmem((16, 8, 128), BF), vmem((128, 2048), BF), vmem((3, 128, 2048), BF), vmem((1, 2048), F32),
             vmem((16, 16, 128), F32), vmem((16, 8, 128), BF), vmem((16, 8, 128), BF),
             vmem((128, 2048), F32), vmem((4, 128, 2048), BF), vmem((4, 64, 192), BF),
             vmem((3, 64, 256), BF), vmem((8, 3, 256, 256), BF), vmem((3, 512, 256), F32),
-            vmem((4, 128, 256), BF), vmem((8, 128, 512), BF), vmem((4, 8, 640), F32),
+            vmem((4, 128, 256), BF), vmem((8, 128, 512), BF), vmem((4, 1, 5), jnp.int32),
             vmem((3, 128, 256), BF), vmem((4, 128, 256), BF),
-            dma((5,)), dma((3,)), dma((3,)), dma((2,)), dma((2,)), dma((3,)), dma((3,)),
+            dma((6,)), dma((3,)), dma((3,)), dma((2,)), dma((2,)), dma((3,)), dma((3,)),
             dma((3, 4)), dma((4,)), dma((3,)), dma((3,)), dma((3,)), dma((3,)),
             dma((2, 7)), dma((2, 7)), dma((2, 4)), dma((2, 4)), dma((2, 8)), dma((2, 8)),
             dma((2, 8)), dma((2, 8)), dma((2,)), dma((2,)), dma((3,)), dma((3,)),
         ],
         compiler_params=pltpu.CompilerParams(
-            collective_id=0, has_side_effects=True, vmem_limit_bytes=66_000_000),
-    )(raw, stream.reshape(128, 2048), conv_w, gain.reshape(1, 2048), w_qkv, mrow)
+            collective_id=0, has_side_effects=True, vmem_limit_bytes=48 * 1024 * 1024),
+    )(*[pltpu.with_memory_space_constraint(a, pltpu.HBM) for a in (
+        raw, stream.reshape(128, 2048), conv_w, gain.reshape(1, 2048), w_qkv, mask.reshape(1, 5))])
     return context.reshape(16, 8, 1024)
 
 

time: 69.9 us -> 67.2 us (0.961)
  local copies, waits for them, and re-layouts: 2.35 us -> 0.71 us
    unnamed x1, local copies, waits for them, and re-layouts: 1.67 us -> 0.71 us
where the time goes in v3:
time: 67.2 us; the launch traced here: 67.1 us
  Pallas kernels  66.4 us (99%)
  local copies, waits for them, and re-layouts  0.71 us (1%)
    pallas_call x1, Pallas kernels, per_device(): pl.pallas_call(layer, out_shape=jax.ShapeDtypeStruct((128, 1024), BF), in...  66.4 us

profile of v3, /device:TPU:1, one launch (start us, length us, event | category | flops | bytes accessed | tf_op | source)
XLA Modules:
  0.0 67.1 jit_solution(9041658674645289)
XLA Ops:
  0.0 66.4 %shard_map.64 = bf16[128,1024]{1,0:T(8,128)(2,1)S(1)} custom-call(bf16[16,8,128]{2,1,0:T(8,128)(2,1)} %raw_h.1, bf16[128,2048]{1,0:T(8,128)(2,1)} %bitcast.5, bf16[3,128,2048]{2,1,0:T(8,128)(2,1)} %conv_h.1, f32[1,2048]{1,0:T(1,128)} %bitcast.6, bf16[64,192]{1,0:T(8,128)(2,1)} %w_h.1, s32[1,5]{1,0:T(1,128)} %bitcast.7), custom_call_target="tpu_custom_call" | custom-call | tf_op jit(solution)/shard_map/pallas_call | solution.py:314
  66.4 0.7 %copy.8 = bf16[16,8,1024]{2,1,0:T(8,128)(2,1)} copy(bf16[16,8,1024]{2,1,0:T(8,128)(2,1)S(1)} %bitcast.4) | data formatting | bytes 524288

commit v4 on v3

--- a/solution.py
+++ b/solution.py
@@ -188,19 +188,22 @@
             spread(way, i).wait_recv()
             pass_on(way, i).start()
 
-    def multiply(i):
+    near, far = 2 * (g // 2), 2 - 2 * (g // 2)
+
+    def multiply(i, first, kind, base, count):
         c = chunk_of(i)
         cols = pl.ds(pl.multiple_of(c * 256, 256), 256)
+        who = pl.ds(base, count)
+        product = jnp.dot(tok[who, :, cols].reshape(128 * count, 256), wfull[c, kind],
+                          preferred_element_type=F32).reshape(count, 128, 256)
+        acc[kind, who] = product if first else acc[kind, who] + product
+
+    def others(i, base, count):
+        lax.fori_loop(1, 3, lambda kind, t: multiply(i, i == 0, kind, base, count), None)
+
+    def landed(i):
         for way in (0, 1):
             pass_on(way, i).wait_recv()
-
-        def one(kind, carry):
-            product = jnp.dot(tok[:, :, cols].reshape(512, 256), wfull[c, kind],
-                              preferred_element_type=F32)
-            acc[kind] = acc[kind] + product if i else product
-            return carry
-
-        lax.fori_loop(0, 3, one, 0)
 
     for kind in (1, 2):
         pltpu.make_async_copy(wp.at[0], quarter(z, kind, x), r_e.at[kind]).wait()
@@ -234,26 +237,38 @@
         else:
             relay(step)
             relay(step + 3)
+        if step == 1:
+            t_partner.wait_recv()
+            landed(0)
+            others(0, near, 2)
         if step == 2:
             t_across.wait_recv()
             t_relay.start()
-            t_partner.wait_recv()
+            landed(1)
+            others(1, near, 2)
+            landed(4)
+            others(4, near, 2)
+    for i in (2, 5):
+        landed(i)
+        others(i, near, 2)
+    relay(7)
     t_relay.wait_recv()
-    for i in (0, 1, 4, 2, 5, 3, 6):
-        multiply(i)
-        if i == 1:
-            relay(7)
-    multiply(7)
+    for i in (0, 1, 4, 2, 5):
+        others(i, far, 2)
+    for i in (3, 6, 7):
+        landed(i)
+        others(i, 0, 4)
 
     for b in range(4):
-        kv[2 + b, :, :256] = acc[1, 128 * b:128 * b + 128].astype(BF)
-        kv[2 + b, :, 256:] = acc[2, 128 * b:128 * b + 128].astype(BF)
+        kv[2 + b, :, :256] = acc[1, b].astype(BF)
+        kv[2 + b, :, 256:] = acc[2, b].astype(BF)
     kv_ahead = send(kv.at[pl.ds(4, 2)], kv.at[pl.ds(0, 2)], s_kv.at[0], r_kv.at[0], (4 * zr + g, depth))
     kv_back = send(kv.at[pl.ds(2, 2)], kv.at[pl.ds(6, 2)], s_kv.at[1], r_kv.at[1], (4 * zl + g, depth))
     kv_ahead.start()
     kv_back.start()
-    for b in range(4):
-        q[b] = acc[0, 128 * b:128 * b + 128].astype(BF)
+    for i in range(8):
+        multiply(i, i == 0, 0, 0, 4)
+    q[...] = acc[0].astype(BF)
     for c in m_copies:
         c.wait()
     kv_ahead.wait()
@@ -320,7 +335,7 @@
             vmem((16, 8, 128), BF), vmem((128, 2048), BF), vmem((3, 128, 2048), BF), vmem((1, 2048), F32),
             vmem((16, 16, 128), F32), vmem((16, 8, 128), BF), vmem((16, 8, 128), BF),
             vmem((128, 2048), F32), vmem((4, 128, 2048), BF), vmem((4, 64, 192), BF),
-            vmem((3, 64, 256), BF), vmem((8, 3, 256, 256), BF), vmem((3, 512, 256), F32),
+            vmem((3, 64, 256), BF), vmem((8, 3, 256, 256), BF), vmem((3, 4, 128, 256), F32),
             vmem((4, 128, 256), BF), vmem((8, 128, 512), BF), vmem((4, 1, 5), jnp.int32),
             vmem((3, 128, 256), BF), vmem((4, 128, 256), BF),
             dma((6,)), dma((3,)), dma((3,)), dma((2,)), dma((2,)), dma((3,)), dma((3,)),

time: 67.2 us -> 65.8 us (0.979)
  Pallas kernels: 66.4 us -> 65 us
    pallas_call x1, Pallas kernels: 66.4 us -> 65 us  [per_device(): pl.pallas_call(layer, out_shape=jax.ShapeDtypeStruct((128, 1024), BF), in...]
where the time goes in v4:
time: 65.8 us; the launch traced here: 65.7 us
  Pallas kernels  65 us (99%)
  local copies, waits for them, and re-layouts  0.71 us (1%)
    pallas_call x1, Pallas kernels, per_device(): pl.pallas_call(layer, out_shape=jax.ShapeDtypeStruct((128, 1024), BF), in...  65 us

profile of v4, /device:TPU:1, one launch (start us, length us, event | category | flops | bytes accessed | tf_op | source)
XLA Modules:
  0.0 65.7 jit_solution(5053496265953828234)
XLA Ops:
  0.0 65.0 %shard_map.64 = bf16[128,1024]{1,0:T(8,128)(2,1)S(1)} custom-call(bf16[16,8,128]{2,1,0:T(8,128)(2,1)} %raw_h.1, bf16[128,2048]{1,0:T(8,128)(2,1)} %bitcast.5, bf16[3,128,2048]{2,1,0:T(8,128)(2,1)} %conv_h.1, f32[1,2048]{1,0:T(1,128)} %bitcast.6, bf16[64,192]{1,0:T(8,128)(2,1)} %w_h.1, s32[1,5]{1,0:T(1,128)} %bitcast.7), custom_call_target="tpu_custom_call" | custom-call | tf_op jit(solution)/shard_map/pallas_call | solution.py:329
  65.0 0.7 %copy.8 = bf16[16,8,1024]{2,1,0:T(8,128)(2,1)} copy(bf16[16,8,1024]{2,1,0:T(8,128)(2,1)S(1)} %bitcast.4) | data formatting | bytes 524288

commit v5 on v4

--- a/solution.py
+++ b/solution.py
@@ -76,7 +76,7 @@
 
     def to_all(j, k):
         pair = 3 * x + j
-        return send(wp.at[j], wfull.at[z, 0, rows], s_d.at[j, k], r_d.at[g],
+        return send(wp.at[j], wfull.at[z, 1, rows], s_d.at[j, k], r_d.at[g],
                     (4 * z + pair % 4, 4 * ((x + k) % 4) + yh))
 
     def to_one(j):
@@ -84,8 +84,8 @@
         return send(wp.at[j], wfull.at[z, pair // 4, rows], s_e.at[j], r_e.at[pair // 4],
                     (4 * z + pair % 4, 4 * g + yh))
 
-    def keep_query(j):
-        return pltpu.make_async_copy(wp.at[j], wfull.at[z, 0, rows], r_d.at[g])
+    def keep_key(j):
+        return pltpu.make_async_copy(wp.at[j], wfull.at[z, 1, rows], r_d.at[g])
 
     def keep_other(j):
         pair = 3 * x + j
@@ -95,20 +95,20 @@
         pair = 3 * x + j
         mine = pair % 4 == g
 
-        @pl.when(pair < 4)
+        @pl.when(pair // 4 == 1)
         def _():
             for k in range(1, 4):
                 act(to_all(j, k))
 
             @pl.when(mine)
             def _():
-                stay(keep_query(j))
+                stay(keep_key(j))
 
             @pl.when(jnp.logical_not(mine))
             def _():
                 act(to_all(j, 0))
 
-        @pl.when(pair >= 4)
+        @pl.when(pair // 4 != 1)
         def _():
             own = jnp.logical_and(mine, x == g)
 
@@ -150,7 +150,7 @@
     t_partner.start()
 
     def half(c, h):
-        return wfull.at[c, 0, pl.ds(128 * h, 128)]
+        return wfull.at[c, 1, pl.ds(128 * h, 128)]
 
     def ring(way, step, h):
         c = (z + 8 - step) % 8 if way == 0 else (z + step) % 8
@@ -161,32 +161,50 @@
     def halves(way, step):
         return (0, 1) if step < 3 else (way,)
 
-    def quarter(c, kinds, at):
-        return wfull.at[c, kinds, pl.ds(pl.multiple_of(64 * at, 64), 64)]
-
-    both = pl.ds(1, 2)
-
-    def narrow(way, step):
+    def part(c, kind, at, start, count):
+        return wfull.at[c, kind, pl.ds(pl.multiple_of(64 * at + start, 32), count)]
+
+    def narrow(kind, way, step):
         c = (z + 8 - step) % 8 if way == 0 else (z + step) % 8
-        part = quarter(c, both if step < 3 else pl.ds(1 + way, 1), x)
-        return send(part, part, s_b.at[way, step], r_b.at[way, step],
+        rows_sent = part(c, kind, x, 0, 64) if step < 3 else part(c, kind, x, 32 * way, 32)
+        return send(rows_sent, rows_sent, s_b.at[kind // 2, way, step], r_b.at[kind // 2, way, step],
                     (4 * (zr if way == 0 else zl) + g, depth))
 
     def chunk_of(i):
         return (z + 8 - i) % 8 if i < 4 else (z + i - 3) % 8
 
-    def spread(way, i):
-        part = quarter(chunk_of(i), both, x)
-        return send(part, part, s_x.at[way, i], r_x.at[way, i], (tm, 4 * (xr if way == 0 else xl) + yh))
-
-    def pass_on(way, i):
-        part = quarter(chunk_of(i), pl.ds(1 + way, 1), xl if way == 0 else xr)
-        return send(part, part, s_f.at[way, i], r_f.at[way, i], (tm, 4 * (xr if way == 0 else xl) + yh))
-
-    def relay(i):
-        for way in (0, 1):
-            spread(way, i).wait_recv()
-            pass_on(way, i).start()
+    def spread(kind, way, i):
+        rows_sent = part(chunk_of(i), kind, x, 0, 64)
+        return send(rows_sent, rows_sent, s_x.at[kind // 2, way, i], r_x.at[kind // 2, way, i],
+                    (tm, 4 * (xr if way == 0 else xl) + yh))
+
+    def pass_on(kind, way, i):
+        rows_sent = part(chunk_of(i), kind, xl if way == 0 else xr, 32 * way, 32)
+        return send(rows_sent, rows_sent, s_f.at[kind // 2, way, i], r_f.at[kind // 2, way, i],
+                    (tm, 4 * (xr if way == 0 else xl) + yh))
+
+    def relay(kind, i):
+        for way in (0, 1):
+            spread(kind, way, i).wait_recv()
+            pass_on(kind, way, i).start()
+
+    def advance(kind, step):
+        for way in (0, 1):
+            narrow(kind, way, step).wait_recv()
+            if step < 3:
+                narrow(kind, way, step + 1).start()
+                for to in (0, 1):
+                    spread(kind, to, (1 if way == 0 else 4) + step).start()
+        if step == 3:
+            for to in (0, 1):
+                spread(kind, to, 7).start()
+
+    def enter(kind):
+        pltpu.make_async_copy(wp.at[0], part(z, kind, x, 0, 64), r_e.at[kind]).wait()
+        for way in (0, 1):
+            narrow(kind, way, 0).start()
+        for way in (0, 1):
+            spread(kind, way, 0).start()
 
     near, far = 2 * (g // 2), 2 - 2 * (g // 2)
 
@@ -201,31 +219,19 @@
     def others(i, base, count):
         lax.fori_loop(1, 3, lambda kind, t: multiply(i, i == 0, kind, base, count), None)
 
-    def landed(i):
-        for way in (0, 1):
-            pass_on(way, i).wait_recv()
-
-    for kind in (1, 2):
-        pltpu.make_async_copy(wp.at[0], quarter(z, kind, x), r_e.at[kind]).wait()
-    for way in (0, 1):
-        narrow(way, 0).start()
-    for way in (0, 1):
-        spread(way, 0).start()
+    def landed(kind, i):
+        for way in (0, 1):
+            pass_on(kind, way, i).wait_recv()
+
+    enter(2)
     for i in range(4):
-        pltpu.make_async_copy(wp.at[0], wfull.at[z, 0, pl.ds(64 * i, 64)], r_d.at[i]).wait()
+        pltpu.make_async_copy(wp.at[0], wfull.at[z, 1, pl.ds(64 * i, 64)], r_d.at[i]).wait()
     for h in (0, 1):
         for way in (0, 1):
             ring(way, 0, h).start()
+    enter(0)
     for step in range(4):
-        for way in (0, 1):
-            narrow(way, step).wait_recv()
-            if step < 3:
-                narrow(way, step + 1).start()
-                for to in (0, 1):
-                    spread(to, (1 if way == 0 else 4) + step).start()
-        if step == 3:
-            for to in (0, 1):
-                spread(to, 7).start()
+        advance(2, step)
         for h in (0, 1):
             for way in (0, 1):
                 if h in halves(way, step):
@@ -233,30 +239,36 @@
                     if step < 3 and h in halves(way, step + 1):
                         ring(way, step + 1, h).start()
         if step == 0:
-            relay(0)
+            relay(2, 0)
         else:
-            relay(step)
-            relay(step + 3)
+            relay(2, step)
+            relay(2, step + 3)
+        advance(0, step)
         if step == 1:
+            relay(0, 0)
             t_partner.wait_recv()
-            landed(0)
+            landed(2, 0)
             others(0, near, 2)
         if step == 2:
+            relay(0, 1)
+            relay(0, 4)
             t_across.wait_recv()
             t_relay.start()
-            landed(1)
+            landed(2, 1)
             others(1, near, 2)
-            landed(4)
+            landed(2, 4)
             others(4, near, 2)
+    relay(2, 7)
+    relay(0, 2)
+    relay(0, 5)
     for i in (2, 5):
-        landed(i)
+        landed(2, i)
         others(i, near, 2)
-    relay(7)
     t_relay.wait_recv()
     for i in (0, 1, 4, 2, 5):
         others(i, far, 2)
     for i in (3, 6, 7):
-        landed(i)
+        landed(2, i)
         others(i, 0, 4)
 
     for b in range(4):
@@ -266,7 +278,10 @@
     kv_back = send(kv.at[pl.ds(2, 2)], kv.at[pl.ds(6, 2)], s_kv.at[1], r_kv.at[1], (4 * zl + g, depth))
     kv_ahead.start()
     kv_back.start()
-    for i in range(8):
+    for i in (3, 6, 7):
+        relay(0, i)
+    for i in (0, 1, 4, 2, 5, 3, 6, 7):
+        landed(0, i)
         multiply(i, i == 0, 0, 0, 4)
     q[...] = acc[0].astype(BF)
     for c in m_copies:
@@ -313,10 +328,12 @@
         for step in range(4):
             for h in halves(way, step):
                 ring(way, step, h).wait_send()
-            narrow(way, step).wait_send()
+            for kind in (0, 2):
+                narrow(kind, way, step).wait_send()
         for i in range(8):
-            spread(way, i).wait_send()
-            pass_on(way, i).wait_send()
+            for kind in (0, 2):
+                spread(kind, way, i).wait_send()
+                pass_on(kind, way, i).wait_send()
     for k in (2, 3, 1):
         give(k).wait()
     for i in range(4):
@@ -340,8 +357,8 @@
             vmem((3, 128, 256), BF), vmem((4, 128, 256), BF),
             dma((6,)), dma((3,)), dma((3,)), dma((2,)), dma((2,)), dma((3,)), dma((3,)),
             dma((3, 4)), dma((4,)), dma((3,)), dma((3,)), dma((3,)), dma((3,)),
-            dma((2, 7)), dma((2, 7)), dma((2, 4)), dma((2, 4)), dma((2, 8)), dma((2, 8)),
-            dma((2, 8)), dma((2, 8)), dma((2,)), dma((2,)), dma((3,)), dma((3,)),
+            dma((2, 7)), dma((2, 7)), dma((2, 2, 4)), dma((2, 2, 4)), dma((2, 2, 8)), dma((2, 2, 8)),
+            dma((2, 2, 8)), dma((2, 2, 8)), dma((2,)), dma((2,)), dma((3,)), dma((3,)),
         ],
         compiler_params=pltpu.CompilerParams(
             collective_id=0, has_side_effects=True, vmem_limit_bytes=48 * 1024 * 1024),

time: 65.8 us -> 66.9 us (1.017)
  Pallas kernels: 65 us -> 66.1 us
    pallas_call x1, Pallas kernels: 65 us -> 66.1 us  [per_device(): pl.pallas_call(layer, out_shape=jax.ShapeDtypeStruct((128, 1024), BF), in...]
where the time goes in v5:
time: 66.9 us; the launch traced here: 66.8 us
  Pallas kernels  66.1 us (99%)
  local copies, waits for them, and re-layouts  0.71 us (1%)
    pallas_call x1, Pallas kernels, per_device(): pl.pallas_call(layer, out_shape=jax.ShapeDtypeStruct((128, 1024), BF), in...  66.1 us

profile of v5, /device:TPU:1, one launch (start us, length us, event | category | flops | bytes accessed | tf_op | source)
XLA Modules:
  0.0 66.8 jit_solution(7235053197829347875)
XLA Ops:
  0.0 66.1 %shard_map.64 = bf16[128,1024]{1,0:T(8,128)(2,1)S(1)} custom-call(bf16[16,8,128]{2,1,0:T(8,128)(2,1)} %raw_h.1, bf16[128,2048]{1,0:T(8,128)(2,1)} %bitcast.5, bf16[3,128,2048]{2,1,0:T(8,128)(2,1)} %conv_h.1, f32[1,2048]{1,0:T(1,128)} %bitcast.6, bf16[64,192]{1,0:T(8,128)(2,1)} %w_h.1, s32[1,5]{1,0:T(1,128)} %bitcast.7), custom_call_target="tpu_custom_call" | custom-call | tf_op jit(solution)/shard_map/pallas_call | solution.py:346
  66.1 0.7 %copy.8 = bf16[16,8,1024]{2,1,0:T(8,128)(2,1)} copy(bf16[16,8,1024]{2,1,0:T(8,128)(2,1)S(1)} %bitcast.4) | data formatting | bytes 524288

commit v6 on v4

--- a/solution.py
+++ b/solution.py
@@ -15,7 +15,7 @@
 
 def layer(raw_h, stream_h, conv_h, gain_h, w_h, mask_h, out, raw, stream, conv, gain, pad, rleft, rright,
           emb, tok, wy, wp, wfull, acc, q, kv, masks, ctx_out, ctx_in, s_in, s_w, r_w, s_raw, r_raw,
-          s_m, r_m, s_d, r_d, s_e, r_e, s_t, r_t, s_z, r_z, s_b, r_b, s_x, r_x, s_f, r_f, s_kv, r_kv,
+          s_m, r_m, s_d, r_d, s_e, r_e, s_t, r_t, s_z, r_z, s_b, r_b, s_x, r_x, s_f, r_f, s_l, r_l, s_kv, r_kv,
           s_c, r_c):
     tm, depth = lax.axis_index("tm"), lax.axis_index("depth")
     z, g = tm // 4, tm % 4
@@ -183,6 +183,10 @@
         part = quarter(chunk_of(i), pl.ds(1 + way, 1), xl if way == 0 else xr)
         return send(part, part, s_f.at[way, i], r_f.at[way, i], (tm, 4 * (xr if way == 0 else xl) + yh))
 
+    def leap():
+        part = quarter(chunk_of(7), both, x)
+        return send(part, part, s_l.at[0], r_l.at[0], (tm, 4 * ((x + 2) % 4) + yh))
+
     def relay(i):
         for way in (0, 1):
             spread(way, i).wait_recv()
@@ -224,6 +228,7 @@
                 for to in (0, 1):
                     spread(to, (1 if way == 0 else 4) + step).start()
         if step == 3:
+            leap().start()
             for to in (0, 1):
                 spread(to, 7).start()
         for h in (0, 1):
@@ -242,22 +247,25 @@
             landed(0)
             others(0, near, 2)
         if step == 2:
-            t_across.wait_recv()
-            t_relay.start()
             landed(1)
             others(1, near, 2)
             landed(4)
             others(4, near, 2)
+    t_across.wait_recv()
+    t_relay.start()
     for i in (2, 5):
         landed(i)
         others(i, near, 2)
-    relay(7)
     t_relay.wait_recv()
     for i in (0, 1, 4, 2, 5):
         others(i, far, 2)
-    for i in (3, 6, 7):
+    for i in (3, 6):
         landed(i)
         others(i, 0, 4)
+    for way in (0, 1):
+        spread(way, 7).wait_recv()
+    leap().wait_recv()
+    others(7, 0, 4)
 
     for b in range(4):
         kv[2 + b, :, :256] = acc[1, b].astype(BF)
@@ -316,7 +324,9 @@
             narrow(way, step).wait_send()
         for i in range(8):
             spread(way, i).wait_send()
-            pass_on(way, i).wait_send()
+            if i < 7:
+                pass_on(way, i).wait_send()
+    leap().wait_send()
     for k in (2, 3, 1):
         give(k).wait()
     for i in range(4):
@@ -341,7 +351,7 @@
             dma((6,)), dma((3,)), dma((3,)), dma((2,)), dma((2,)), dma((3,)), dma((3,)),
             dma((3, 4)), dma((4,)), dma((3,)), dma((3,)), dma((3,)), dma((3,)),
             dma((2, 7)), dma((2, 7)), dma((2, 4)), dma((2, 4)), dma((2, 8)), dma((2, 8)),
-            dma((2, 8)), dma((2, 8)), dma((2,)), dma((2,)), dma((3,)), dma((3,)),
+            dma((2, 7)), dma((2, 7)), dma((1,)), dma((1,)), dma((2,)), dma((2,)), dma((3,)), dma((3,)),
         ],
         compiler_params=pltpu.CompilerParams(
             collective_id=0, has_side_effects=True, vmem_limit_bytes=48 * 1024 * 1024),

time: 65.8 us -> 68.1 us (1.035)
  Pallas kernels: 65 us -> 67.3 us
    pallas_call x1, Pallas kernels: 65 us -> 67.3 us  [per_device(): pl.pallas_call(layer, out_shape=jax.ShapeDtypeStruct((128, 1024), BF), in...]
where the time goes in v6:
time: 68.1 us; the launch traced here: 68 us
  Pallas kernels  67.3 us (99%)
  local copies, waits for them, and re-layouts  0.71 us (1%)
    pallas_call x1, Pallas kernels, per_device(): pl.pallas_call(layer, out_shape=jax.ShapeDtypeStruct((128, 1024), BF), in...  67.3 us

profile of v6, /device:TPU:1, one launch (start us, length us, event | category | flops | bytes accessed | tf_op | source)
XLA Modules:
  0.0 68.0 jit_solution(6659906204860208743)
XLA Ops:
  0.0 67.3 %shard_map.64 = bf16[128,1024]{1,0:T(8,128)(2,1)S(1)} custom-call(bf16[16,8,128]{2,1,0:T(8,128)(2,1)} %raw_h.1, bf16[128,2048]{1,0:T(8,128)(2,1)} %bitcast.5, bf16[3,128,2048]{2,1,0:T(8,128)(2,1)} %conv_h.1, f32[1,2048]{1,0:T(1,128)} %bitcast.6, bf16[64,192]{1,0:T(8,128)(2,1)} %w_h.1, s32[1,5]{1,0:T(1,128)} %bitcast.7), custom_call_target="tpu_custom_call" | custom-call | tf_op jit(solution)/shard_map/pallas_call | solution.py:339
  67.3 0.7 %copy.8 = bf16[16,8,1024]{2,1,0:T(8,128)(2,1)} copy(bf16[16,8,1024]{2,1,0:T(8,128)(2,1)S(1)} %bitcast.4) | data formatting | bytes 524288

commit v7 on v4

--- a/solution.py
+++ b/solution.py
@@ -143,10 +143,16 @@
     tok[g] = (emb[...] * inv * gain[...]).astype(BF)
     partner = g + 1 - 2 * (g % 2)
     across = (g + 2) % 4
-    t_across = send(tok.at[g], tok.at[g], s_t.at[0], r_t.at[0], (4 * z + across, depth))
-    t_partner = send(tok.at[g], tok.at[g], s_t.at[1], r_t.at[1], (4 * z + partner, depth))
-    t_relay = send(tok.at[across], tok.at[across], s_t.at[2], r_t.at[2], (4 * z + partner, depth))
-    t_across.start()
+    t_partner = send(tok.at[g], tok.at[g], s_t.at[4], r_t.at[4], (4 * z + partner, depth))
+
+    def piece(i, i_sem, whose, to):
+        rows_sent = tok.at[whose, pl.ds(64 * i, 64)]
+        return send(rows_sent, rows_sent, s_t.at[i_sem + i], r_t.at[i_sem + i], (4 * z + to, depth))
+
+    t_across = [piece(i, 0, g, across) for i in range(2)]
+    t_relay = [piece(i, 2, across, partner) for i in range(2)]
+    for c in t_across:
+        c.start()
     t_partner.start()
 
     def half(c, h):
@@ -242,17 +248,20 @@
             landed(0)
             others(0, near, 2)
         if step == 2:
-            t_across.wait_recv()
-            t_relay.start()
             landed(1)
             others(1, near, 2)
+            t_across[0].wait_recv()
+            t_relay[0].start()
             landed(4)
             others(4, near, 2)
+            t_across[1].wait_recv()
+            t_relay[1].start()
     for i in (2, 5):
         landed(i)
         others(i, near, 2)
     relay(7)
-    t_relay.wait_recv()
+    for c in t_relay:
+        c.wait_recv()
     for i in (0, 1, 4, 2, 5):
         others(i, far, 2)
     for i in (3, 6, 7):
@@ -306,9 +315,8 @@
 
     for j in range(3):
         direct(j, lambda c: c.wait_send(), lambda c: None)
-    t_across.wait_send()
-    t_partner.wait_send()
-    t_relay.wait_send()
+    for c in t_across + t_relay + [t_partner]:
+        c.wait_send()
     for way in (0, 1):
         for step in range(4):
             for h in halves(way, step):
@@ -339,7 +347,7 @@
             vmem((4, 128, 256), BF), vmem((8, 128, 512), BF), vmem((4, 1, 5), jnp.int32),
             vmem((3, 128, 256), BF), vmem((4, 128, 256), BF),
             dma((6,)), dma((3,)), dma((3,)), dma((2,)), dma((2,)), dma((3,)), dma((3,)),
-            dma((3, 4)), dma((4,)), dma((3,)), dma((3,)), dma((3,)), dma((3,)),
+            dma((3, 4)), dma((4,)), dma((3,)), dma((3,)), dma((5,)), dma((5,)),
             dma((2, 7)), dma((2, 7)), dma((2, 4)), dma((2, 4)), dma((2, 8)), dma((2, 8)),
             dma((2, 8)), dma((2, 8)), dma((2,)), dma((2,)), dma((3,)), dma((3,)),
         ],

time: 65.8 us -> 65.8 us (level)
  no operation moved by 1% of the time
where the time goes in v7:
time: 65.8 us; the launch traced here: 65.7 us
  Pallas kernels  65 us (99%)
  local copies, waits for them, and re-layouts  0.71 us (1%)
    pallas_call x1, Pallas kernels, per_device(): pl.pallas_call(layer, out_shape=jax.ShapeDtypeStruct((128, 1024), BF), in...  65 us

profile of v7, /device:TPU:1, one launch (start us, length us, event | category | flops | bytes accessed | tf_op | source)
XLA Modules:
  0.0 65.7 jit_solution(16542444828950747395)
XLA Ops:
  0.0 65.0 %shard_map.64 = bf16[128,1024]{1,0:T(8,128)(2,1)S(1)} custom-call(bf16[16,8,128]{2,1,0:T(8,128)(2,1)} %raw_h.1, bf16[128,2048]{1,0:T(8,128)(2,1)} %bitcast.5, bf16[3,128,2048]{2,1,0:T(8,128)(2,1)} %conv_h.1, f32[1,2048]{1,0:T(1,128)} %bitcast.6, bf16[64,192]{1,0:T(8,128)(2,1)} %w_h.1, s32[1,5]{1,0:T(1,128)} %bitcast.7), custom_call_target="tpu_custom_call" | custom-call | tf_op jit(solution)/shard_map/pallas_call | solution.py:337
  65.0 0.7 %copy.8 = bf16[16,8,1024]{2,1,0:T(8,128)(2,1)} copy(bf16[16,8,1024]{2,1,0:T(8,128)(2,1)S(1)} %bitcast.4) | data formatting | bytes 524288

commit v8 on v4

--- a/solution.py
+++ b/solution.py
@@ -199,7 +199,8 @@
         acc[kind, who] = product if first else acc[kind, who] + product
 
     def others(i, base, count):
-        lax.fori_loop(1, 3, lambda kind, t: multiply(i, i == 0, kind, base, count), None)
+        for kind in (1, 2):
+            multiply(i, i == 0, kind, base, count)
 
     def landed(i):
         for way in (0, 1):

time: 65.8 us -> 65.4 us (level)
  no operation moved by 1% of the time
where the time goes in v8:
time: 65.4 us; the launch traced here: 65.2 us
  Pallas kernels  64.5 us (99%)
  local copies, waits for them, and re-layouts  0.71 us (1%)
    pallas_call x1, Pallas kernels, per_device(): pl.pallas_call(layer, out_shape=jax.ShapeDtypeStruct((128, 1024), BF), in...  64.5 us

profile of v8, /device:TPU:1, one launch (start us, length us, event | category | flops | bytes accessed | tf_op | source)
XLA Modules:
  0.0 65.2 jit_solution(7463720083377316793)
XLA Ops:
  0.0 64.5 %shard_map.64 = bf16[128,1024]{1,0:T(8,128)(2,1)S(1)} custom-call(bf16[16,8,128]{2,1,0:T(8,128)(2,1)} %raw_h.1, bf16[128,2048]{1,0:T(8,128)(2,1)} %bitcast.5, bf16[3,128,2048]{2,1,0:T(8,128)(2,1)} %conv_h.1, f32[1,2048]{1,0:T(1,128)} %bitcast.6, bf16[64,192]{1,0:T(8,128)(2,1)} %w_h.1, s32[1,5]{1,0:T(1,128)} %bitcast.7), custom_call_target="tpu_custom_call" | custom-call | tf_op jit(solution)/shard_map/pallas_call | solution.py:330
  64.5 0.7 %copy.8 = bf16[16,8,1024]{2,1,0:T(8,128)(2,1)} copy(bf16[16,8,1024]{2,1,0:T(8,128)(2,1)S(1)} %bitcast.4) | data formatting | bytes 524288
